TPU v7x, 32 devices: a whole 2x2x4 slice. The times are simulated.
32 devices in a mesh: scen: 8 (over z, y), rows: 2 (over x), section: 2 (over core).
Axes of the slice: x: 2, y: 2, z: 4, core: 2. Of those that a mesh axis runs over, the one named last changes fastest.
Arguments:
- lp_blocks: bfloat16 [192, 2, 4, 2, 128, 128], P('scen', 'rows', 'section'), may hold values from -0.1875 to 0.1875
- block_columns: int32 [192, 2, 4, 2], P('scen', None, 'section'), may hold values from 0 to 175
- scenario_nodes: int32 [3, 192], P(None, 'scen'), may hold values from 0 to 511, as said below
- scenario_weights: float32 [192], P('scen'), may hold values from 0.5 to 4.5
- cost: bfloat16 [192, 4, 22528], P('scen', 'section'), may hold values from -6 to 6
- bounds_rhs: float32 [192, 256], P('scen', 'rows'), may hold values from -6 to 6
- primal_start: bfloat16 [192, 4, 22528], P('scen', 'section'), may hold values from 0 to 2
- dual_start: float32 [192, 256], P('scen', 'rows'), may hold values from 0 to 1
- multiplier_start: float32 [192, 4, 512], P('scen', 'section'), may hold values from -3 to 3
- consensus_start: float32 [585, 512], replicated, may hold values from 0 to 2
Outputs:
- primal: float32 [192, 4, 22528], P('scen', 'section')
- dual: float32 [192, 256], P('scen', 'rows')
- multiplier: float32 [192, 4, 512], P('scen', 'section')
- penalty: float32 [], replicated
Inputs may be any that keep to these rules, and one draw needn't show every extreme that they name: `scenario_nodes`: node ids never fall from one scenario to the next at any section; the section-three node is the section-four node // 8 and the section-two node the section-three node // 8; the first scenario lies in node 0 and the last in node 511 of section four.
All inputs are finite; a program needn't handle non-finite values.
Results may differ from a plain program's by a relative error of at most 0.0018.
Values sent between devices are 32-bit elements; how exact they have to be, the bound alone decides.
No kernel may reach another device: no remote copies, remote signals or barrier semaphores. Data moves between devices by JAX's collectives and lax.ppermute only.
A program may use at most 128 MiB of HBM per device.

v0:
```python
import jax
import jax.numpy as jnp
from jax import lax
from jax.sharding import PartitionSpec as P

BLK = 128
CPS = 176
N1 = 8
SWEEPS = 2
N2 = 64
NODES = 585
TAU_STEP = 0.4
SIGMA_STEP = 0.4
RHO_START = 1.0
EPSILON = 1e-06


def averaged(node_table, node_mass):
    positive = node_mass > 0
    safe_mass = jnp.where(positive, node_mass, 1.0)
    return jnp.where(positive[:, None], node_table / safe_mass[:, None], 0.0)


def local(
    lp_blocks,
    block_columns,
    scenario_nodes,
    scenario_weights,
    cost,
    bounds_rhs,
    primal_start,
    dual_start,
    multiplier_start,
    consensus_start,
):
    scenario_count = cost.shape[0]
    local_sections = cost.shape[1]
    columns = cost.shape[2]
    hedged = multiplier_start.shape[2]
    row_blocks = dual_start.shape[1] // BLK
    section_index = lax.axis_index("section")
    row_index = lax.axis_index("rows")
    selector = (block_columns[..., None] == jnp.arange(CPS, dtype=jnp.int32)).astype(jnp.float32)
    local_selector = lax.dynamic_slice_in_dim(
        selector, row_index * row_blocks, row_blocks, 1
    ).astype(jnp.bfloat16)
    offsets = jnp.array([1, 1 + N1, 1 + N1 + N2], jnp.int32)
    node_rows = jnp.concatenate(
        [jnp.zeros((1, scenario_count), jnp.int32), scenario_nodes + offsets[:, None]], axis=0
    )
    local_rows = lax.dynamic_slice_in_dim(
        node_rows, section_index * local_sections, local_sections, 0
    )
    membership = (
        local_rows[:, None, :] == jnp.arange(NODES, dtype=jnp.int32)[None, :, None]
    ).astype(jnp.float32)
    cost_full = cost.astype(jnp.float32)

    def spread(table):
        return jnp.einsum("jns,nc->sjc", membership, table, precision=lax.Precision.HIGHEST)

    penalty = jnp.asarray(RHO_START, jnp.float32)
    primal = primal_start.astype(jnp.float32)
    dual, multiplier, previous = (dual_start, multiplier_start, consensus_start)
    for sweep_index in range(SWEEPS):
        anchors = spread(previous)
        dual_half = dual.reshape(scenario_count, row_blocks, BLK).astype(jnp.bfloat16)
        pieces = jnp.einsum(
            "srjnab,sra->srjnb", lp_blocks, dual_half, preferred_element_type=jnp.float32
        )
        gathered = lax.all_gather(pieces, "rows", axis=1, tiled=True)
        placed = jnp.einsum(
            "srjnc,srjnb->sjcb", selector, gathered, precision=lax.Precision.HIGHEST
        )
        adjoint = placed.reshape(scenario_count, local_sections, columns)
        hedge_term = multiplier + penalty * (primal[:, :, :hedged] - anchors)
        hedge_full = jnp.pad(hedge_term, ((0, 0), (0, 0), (0, columns - hedged)))
        primal_next = jnp.maximum(primal - TAU_STEP * (cost_full + adjoint + hedge_full), 0.0)
        step_half = (2.0 * primal_next - primal).astype(jnp.bfloat16)
        blocks = step_half.reshape(scenario_count, local_sections, CPS, BLK)
        picked = jnp.einsum(
            "srjnc,sjcb->srjnb", local_selector, blocks, preferred_element_type=jnp.float32
        ).astype(jnp.bfloat16)
        image = lax.psum(
            jnp.einsum("srjnab,srjnb->sra", lp_blocks, picked, preferred_element_type=jnp.float32),
            "section",
        )
        dual_next = jnp.maximum(
            dual + SIGMA_STEP * (image.reshape(scenario_count, -1) - bounds_rhs), 0.0
        )
        hedged_next = primal_next[:, :, :hedged]
        weighted = scenario_weights[:, None, None] * hedged_next
        node_table, node_mass = lax.psum(
            (
                jnp.einsum("jns,sjc->nc", membership, weighted, precision=lax.Precision.HIGHEST),
                jnp.einsum(
                    "jns,s->n", membership, scenario_weights, precision=lax.Precision.HIGHEST
                ),
            ),
            "scen",
        )
        consensus = averaged(node_table, node_mass)
        new_anchors = spread(consensus)
        gap_local = jnp.sum(scenario_weights[:, None, None] * (hedged_next - new_anchors) ** 2)
        drift_local = jnp.sum(scenario_weights[:, None, None] * (new_anchors - anchors) ** 2)
        primal_gap, drift_gap = lax.psum((gap_local, drift_local), ("scen", "section"))
        multiplier = multiplier + penalty * (hedged_next - new_anchors)
        penalty = penalty * jnp.sqrt(primal_gap / (drift_gap + EPSILON))
        primal, dual, previous = (primal_next, dual_next, consensus)
    return (primal, dual, multiplier, penalty)


def solution(mesh):
    in_specs = (
        P("scen", "rows", "section", None, None, None),
        P("scen", None, "section", None),
        P(None, "scen"),
        P("scen"),
        P("scen", "section", None),
        P("scen", "rows"),
        P("scen", "section", None),
        P("scen", "rows"),
        P("scen", "section", None),
        P(),
    )
    out_specs = (P("scen", "section", None), P("scen", "rows"), P("scen", "section", None), P())
    return jax.shard_map(local, mesh=mesh, in_specs=in_specs, out_specs=out_specs, check_vma=False)
```

profile of v0, /device:TPU:0, one launch (start us, length us, event | category | flops | bytes accessed | tf_op | source)
XLA Modules:
  0.0 297.4 jit_solution(1320190035164285401)
XLA Ops:
  8.1 1.0 copy-done
  9.7 5.7 %all-gather = f32[24,4,2,128]{3,0,2,1:T(8,128)S(1)} all-gather(f32[24,2,2,128]{3,0,2,1:T(8,128)S(1)} %bitcast.114), channel_id=2, replica_groups=mesh['scen'=8,'rows'=2,'section'=2] {'rows'}, dimensions={1}, use_global_device_ids=true | all-gather | bytes 147456 | tf_op jit(solution)/shard_map/all_gather | solution.py:71
  15.4 3.8 %fusion.53 = f32[24,2,176,128,1]{3,2,1,0,4:T(8,128)S(1)} fusion(f32[24,2,2,2,128]{4,0,3,2,1:T(8,128)S(1)} %bitcast.113, s32[24,2,2,2]{3,2,0,1:T(2,128)S(1)} %copy.45), kind=kOutput, calls=%fused_computation.58 | convolution fusion | flops 51938304 | bytes 4424448 | tf_op jit(solution)/shard_map/srjnc,srjnb->sjcb/dot_general | solution.py:72
  19.2 2.4 copy.119
  21.6 5.4 %reshape.65 = f32[24,2,22528]{2,0,1:T(8,128)} reshape(f32[24,2,176,128]{3,2,0,1:T(8,128)} %bitcast.103) | data formatting | bytes 8650752 | tf_op jit(solution)/shard_map/reshape | solution.py:75
  26.9 4.4 %copy_convert_fusion = f32[24,2,22528]{2,0,1:T(8,128)} fusion(bf16[24,2,22528]{2,1,0:T(2,128)(2,1)} %param.17), kind=kLoop, calls=%fused_computation.26 | loop fusion | flops 1081344 | bytes 6488064 | tf_op jit(solution)/shard_map/convert_element_type | solution.py:63
  31.4 1.9 fusion.50
  33.3 5.4 %subtract_convert_fusion.1 = (bf16[24,2,22528]{2,0,1:T(8,128)(2,1)}, f32[24,2,22528]{2,0,1:T(8,128)S(1)}) fusion(bf16[24,2,22528]{2,1,0:T(2,128)(2,1)} %param.17, f32[24,2,512]{2,0,1:T(8,128)S(1)} %get-tuple-element.29, f32[24,2,22528]{2,0,1:T(8,128)} %reshape.65, bf16[24,2,22528]{2,1,0:T(2,128)(2,1)} %param.15), kind=kLoop, calls=%fused_computation.13 | loop fusion | flops 10813440 | bytes 15237120 | tf_op jit(solution)/shard_map/convert_element_type | solution.py:79
  38.7 2.0 copy-done.1
  40.7 1.8 convolution_bitcast_fusion.1
  42.8 3.3 %copy.72 = bf16[6,8,176,128]{3,2,1,0:T(8,128)(2,1)} copy(bf16[6,8,176,128]{3,1,2,0:T(8,128)(2,1)} %bitcast.106) | data formatting | bytes 4325376
  46.1 2.3 fusion.40
  49.3 3.3 %psum.66 = f32[24,128]{1,0:T(8,128)S(1)} all-reduce(f32[24,128]{1,0:T(8,128)S(1)} %bitcast.117), channel_id=1, replica_groups=mesh['scen'=8,'rows'=2,'section'=2] {'section'}, use_global_device_ids=true, to_apply=%region_0.1 | all-reduce | flops 3072 | bytes 24576 | tf_op jit(solution)/shard_map/psum | solution.py:84
  53.2 5.1 %all-gather.1 = f32[24,4,2,128]{3,0,2,1:T(8,128)S(1)} all-gather(f32[24,2,2,128]{3,0,2,1:T(8,128)S(1)} %bitcast.115), channel_id=3, replica_groups=mesh['scen'=8,'rows'=2,'section'=2] {'rows'}, dimensions={1}, use_global_device_ids=true | all-gather | bytes 147456 | tf_op jit(solution)/shard_map/all_gather | solution.py:71
  58.3 3.8 %fusion.51 = f32[24,2,176,128,1]{3,2,1,0,4:T(8,128)S(1)} fusion(f32[24,2,2,2,128]{4,0,3,2,1:T(8,128)S(1)} %bitcast.112, s32[24,2,2,2]{3,2,0,1:T(2,128)S(1)} %copy.45), kind=kOutput, calls=%fused_computation.56 | convolution fusion | flops 51938304 | bytes 4424448 | tf_op jit(solution)/shard_map/srjnc,srjnb->sjcb/dot_general | solution.py:72
  62.1 2.4 copy.118
  64.5 5.4 %reshape.70 = f32[24,2,22528]{2,0,1:T(8,128)} reshape(f32[24,2,176,128]{3,2,0,1:T(8,128)} %bitcast.104) | data formatting | bytes 8650752 | tf_op jit(solution)/shard_map/reshape | solution.py:75
  70.2 22.1 %psum.67 = f32[585]{0:T(1024)S(1)} all-reduce(f32[585]{0:T(1024)S(1)} %convolution_reduce_fusion), channel_id=1, replica_groups=mesh['scen'=8,'rows'=2,'section'=2] {'scen'}, use_global_device_ids=true, to_apply=%region_2.3 | all-reduce | flops 585 | bytes 4680 | tf_op jit(solution)/shard_map/psum | solution.py:93
  92.3 33.4 %all-reduce.8.cloned.1.call-done = f32[585,512]{1,0:T(8,128)} async-done(((f32[585,512]{1,0:T(8,128)}), f32[585,512]{1,0:T(8,128)}) %all-reduce.8.cloned.1.call-update) | async-done | bytes 1198096 | tf_op jit(solution)/shard_map/psum | solution.py:93
  125.8 2.1 fusion.25
  127.8 1.6 multiply_reduce_fusion.2
  129.4 31.8 %all-reduce.4 = (f32[]{:T(128)}, f32[]{:T(128)}) all-reduce(f32[]{:T(128)} %get-tuple-element.19, f32[]{:T(128)} %get-tuple-element.18), channel_id=1, replica_groups=mesh['scen'=8,'rows'=2,'section'=2] {'scen','section'}, use_global_device_ids=true, to_apply=%region_5.6 | all-reduce | flops 2 | bytes 16 | tf_op jit(solution)/shard_map/psum | solution.py:106
  162.6 0.9 multiply_add_fusion.1
  163.5 5.7 %subtract_convert_fusion = (bf16[24,2,22528]{2,0,1:T(8,128)(2,1)}, f32[24,2,22528]{2,0,1:T(8,128)S(1)}) fusion(f32[24,2,22528]{2,0,1:T(8,128)} %copy-done.1, f32[24,2,512]{2,0,1:T(8,128)S(1)} %multiply_add_fusion.1, f32[24,2,22528]{2,0,1:T(8,128)} %reshape.70, bf16[24,2,22528]{2,1,0:T(2,128)(2,1)} %param.15), kind=kLoop, calls=%fused_computation.12 | loop fusion | flops 9732096 | bytes 17399808 | tf_op jit(solution)/shard_map/convert_element_type | solution.py:79
  169.3 2.0 copy-done.2
  171.3 1.8 convolution_bitcast_fusion
  173.1 7.8 %copy.54 = f32[24,2,22528]{2,1,0:T(2,128)} copy(f32[24,2,22528]{2,0,1:T(8,128)} %copy-done.2) | data formatting | bytes 8650752
  183.4 3.3 %psum.71 = f32[24,128]{1,0:T(8,128)S(1)} all-reduce(f32[24,128]{1,0:T(8,128)S(1)} %bitcast.118), channel_id=1, replica_groups=mesh['scen'=8,'rows'=2,'section'=2] {'section'}, use_global_device_ids=true, to_apply=%region_8.9 | all-reduce | flops 3072 | bytes 24576 | tf_op jit(solution)/shard_map/psum | solution.py:84
  187.3 64.4 %all-reduce.10.cloned.1.call-done = f32[585,512]{1,0:T(8,128)} async-done(((f32[585,512]{1,0:T(8,128)}), f32[585,512]{1,0:T(8,128)}) %all-reduce.10.cloned.1.call-update) | async-done | bytes 1198096 | tf_op jit(solution)/shard_map/psum | solution.py:93
  251.7 2.1 fusion.22
  253.8 1.7 multiply_reduce_fusion
  256.2 31.9 %all-reduce.3 = (f32[]{:T(128)}, f32[]{:T(128)}) all-reduce(f32[]{:T(128)} %get-tuple-element.17, f32[]{:T(128)} %get-tuple-element.16), channel_id=1, replica_groups=mesh['scen'=8,'rows'=2,'section'=2] {'scen','section'}, use_global_device_ids=true, to_apply=%region_11.12 | all-reduce | flops 2 | bytes 16 | tf_op jit(solution)/shard_map/psum | solution.py:106
  (52 shorter events, 7.5 us)
Async XLA Ops:
  7.2 1.9 copy-start
  7.2 2.4 copy-start.12
  7.2 118.6 %all-reduce.8.cloned.1.call-start = ((), (), s32[]{:S(2)}) async-start(), calls=%async_computation | async-start | bytes 2424832 | tf_op jit(solution)/shard_map/psum | solution.py:93
  26.9 4.4 %copy-start.13 = (s32[3,24]{1,0:T(4,128)S(1)}, s32[3,24]{1,0:T(4,128)}, u32[]{:S(2)}) copy-start(s32[3,24]{1,0:T(4,128)} %param.13) | copy-start | bytes 868
  26.9 4.4 %copy-start.14 = (s32[3]{0:T(128)S(1)}, s32[3]{0:T(128)}, u32[]{:S(2)}) copy-start(s32[3]{0:T(128)} %constant.8.clone) | copy-start | bytes 40
  26.9 4.5 %copy-start.4 = (f32[24,2,512]{2,1,0:T(2,128)S(1)}, f32[24,2,512]{2,1,0:T(2,128)}, u32[]{:S(2)}) copy-start(f32[24,2,512]{2,1,0:T(2,128)} %param.19) | copy-start | bytes 294916
  33.3 7.4 %copy-start.10 = (f32[24]{0:T(128)S(1)}, f32[24]{0:T(128)}, u32[]{:S(2)}) copy-start(f32[24]{0:T(128)} %param.14) | copy-start | bytes 292
  38.7 2.0 copy-start.1
  42.5 209.2 %all-reduce.10.cloned.1.call-start = ((), (), s32[]{:S(2)}) async-start(), calls=%async_computation.1 | async-start | bytes 2424832 | tf_op jit(solution)/shard_map/psum | solution.py:93
  42.8 5.6 %copy-start.6 = (pred[24,2,2,2,176]{4,3,2,0,1:T(4,128)(4,1)}, pred[24,2,2,2,176]{4,3,2,0,1:T(4,128)(4,1)S(1)}, u32[]{:S(2)}) copy-start(pred[24,2,2,2,176]{4,3,2,0,1:T(4,128)(4,1)S(1)} %iota_compare_fusion) | copy-start | bytes 101380
  46.1 6.5 %copy-start.5 = (f32[24,128]{1,0:T(8,128)S(1)}, f32[24,128]{1,0:T(8,128)}, u32[]{:S(2)}) copy-start(f32[24,128]{1,0:T(8,128)} %param.18) | copy-start | bytes 36868
  46.1 6.5 %copy-start.8 = (f32[24,128]{1,0:T(8,128)S(1)}, f32[24,128]{1,0:T(8,128)}, u32[]{:S(2)}) copy-start(f32[24,128]{1,0:T(8,128)} %param.16) | copy-start | bytes 36868
  64.5 5.5 %copy-start.11 = (f32[24]{0:T(128)S(1)}, f32[24]{0:T(128)}, u32[]{:S(2)}) copy-start(f32[24]{0:T(128)} %param.14) | copy-start | bytes 292
  169.3 2.0 copy-start.2
  173.1 7.8 %copy-start.3 = (bf16[24,2,22528]{2,0,1:T(8,128)(2,1)S(1)}, bf16[24,2,22528]{2,0,1:T(8,128)(2,1)}, u32[]{:S(2)}) copy-start(bf16[24,2,22528]{2,0,1:T(8,128)(2,1)} %get-tuple-element.24) | copy-start | bytes 6488068
  180.9 0.9 copy-start.7
  181.8 4.9 %copy-start.9 = (f32[24,128]{1,0:T(8,128)S(1)}, f32[24,128]{1,0:T(8,128)}, u32[]{:S(2)}) copy-start(f32[24,128]{1,0:T(8,128)} %param.16) | copy-start | bytes 36868
Sparse Core Ops, SparseCore 0:
  42.7 83.0 all-reduce.7
  173.3 78.4 all-reduce.9
where the time goes:
time: 298 us; the launch traced here: 297 us
  blocking collectives  103 us (35%)
  waiting for transfers between devices  97.9 us (33%)
  local copies, waits for them, and re-layouts  33.3 us (11%)
  matrix products  23.3 us (8%)
  other arithmetic  21.6 us (7%)
  between operations  18.1 us (6%)
    psum x2, waiting for transfers between devices, local(): lax.psum((jnp.einsum('jns,sjc->nc', membership, weighted, precision=lax.P...  97.8 us
    psum x2, blocking collectives, local(): lax.psum((gap_local, drift_local), ('scen', 'section'))  63.7 us
    psum x1, blocking collectives, local(): lax.psum((jnp.einsum('jns,sjc->nc', membership, weighted, precision=lax.P...  22.1 us
    unnamed x35, local copies, waits for them, and re-layouts  17.8 us
    convert_element_type x2, other arithmetic, local(): step_half = (2.0 * primal_next - primal).astype(jnp.bfloat16)  11.1 us
    reshape x2, local copies, waits for them, and re-layouts, local(): adjoint = placed.reshape(scenario_count, local_sections, columns)  10.8 us
    all_gather x2, blocking collectives, local(): gathered = lax.all_gather(pieces, 'rows', axis=1, tiled=True)  10.8 us
    dot_general x2, matrix products, local(): jnp.einsum('srjnc,srjnb->sjcb', selector, gathered, precision=lax.Precisi...  7.67 us
  transfers between devices with their start and end apart: 2, of which 2 were waited for; matrix products, arithmetic and copies ran while one was open for 10% of the time, Pallas kernels for 0%

commit v1 on v0

--- a/solution.py
+++ b/solution.py
@@ -13,6 +13,18 @@
 SIGMA_STEP = 0.4
 RHO_START = 1.0
 EPSILON = 1e-06
+
+
+def ring_product(x, axis, dim, term):
+    size, position = (lax.axis_size(axis), lax.axis_index(axis))
+    downward = [(i, (i - 1) % size) for i in range(size)]
+    rows = x.shape[dim]
+    held = x
+    total = term(held, position * rows)
+    for step in range(1, size):
+        held = lax.ppermute(held, axis, downward)
+        total = total + term(held, (position + step) % size * rows)
+    return total
 
 
 def averaged(node_table, node_mass):
@@ -68,9 +80,16 @@
         pieces = jnp.einsum(
             "srjnab,sra->srjnb", lp_blocks, dual_half, preferred_element_type=jnp.float32
         )
-        gathered = lax.all_gather(pieces, "rows", axis=1, tiled=True)
-        placed = jnp.einsum(
-            "srjnc,srjnb->sjcb", selector, gathered, precision=lax.Precision.HIGHEST
+        placed = ring_product(
+            pieces,
+            "rows",
+            1,
+            lambda shard, start: jnp.einsum(
+                "srjnc,srjnb->sjcb",
+                lax.dynamic_slice_in_dim(selector, start, shard.shape[1], axis=1),
+                shard,
+                precision=lax.Precision.HIGHEST,
+            ),
         )
         adjoint = placed.reshape(scenario_count, local_sections, columns)
         hedge_term = multiplier + penalty * (primal[:, :, :hedged] - anchors)

time: 298 us -> 331 us (1.11)
  waiting for transfers between devices: 97.9 us -> 125 us
  matrix products: 23.3 us -> 39.2 us
  blocking collectives: 103 us -> 92 us
  local copies, waits for them, and re-layouts: 33.3 us -> 25.6 us
  other arithmetic: 21.6 us -> 26.4 us
  starting transfers between devices: 0.08 us -> 3.59 us
    psum x2, waiting for transfers between devices: 97.8 us -> 125 us  [local(): lax.psum((jnp.einsum('jns,sjc->nc', membership, weighted, precision=lax.P...]
    dot_general x2 -> x4, matrix products: 7.67 us -> 24.1 us  [local(): jnp.einsum('srjnc,srjnb->sjcb', lax.dynamic_slice_in_dim(selector, start,...]
    all_gather x2 -> x0, blocking collectives: 10.8 us -> none  [local(): gathered = lax.all_gather(pieces, 'rows', axis=1, tiled=True)]
    unnamed x35 -> x45, local copies, waits for them, and re-layouts: 17.8 us -> 12.2 us
    dot_general x4 -> x0, local copies, waits for them, and re-layouts: 4.73 us -> none  [the longest x2 4.72 us: local(): jnp.einsum('srjnc,srjnb->sjcb', selector, gathered, precision=lax.Precisi...]
    ppermute x0 -> x2, starting transfers between devices: none -> 3.51 us  [ring_product(): held = lax.ppermute(held, axis, downward)]
  transfers between devices with their start and end apart: 2 -> 4, of which waited for: 2 -> 2; matrix products, arithmetic and copies ran while one was open for 10% -> 13% of each run, Pallas kernels for 0% -> 0%
where the time goes in v1:
time: 331 us; the launch traced here: 330 us
  waiting for transfers between devices  125 us (38%)
  blocking collectives  92 us (28%)
  matrix products  39.2 us (12%)
  other arithmetic  26.4 us (8%)
  local copies, waits for them, and re-layouts  25.6 us (8%)
  between operations  18.2 us (5%)
  starting transfers between devices  3.59 us (1%)
    psum x2, waiting for transfers between devices, local(): lax.psum((jnp.einsum('jns,sjc->nc', membership, weighted, precision=lax.P...  125 us
    psum x2, blocking collectives, local(): lax.psum((gap_local, drift_local), ('scen', 'section'))  63.7 us
    dot_general x4, matrix products, local(): jnp.einsum('srjnc,srjnb->sjcb', lax.dynamic_slice_in_dim(selector, start,...  24.1 us
    psum x1, blocking collectives, local(): lax.psum((jnp.einsum('jns,sjc->nc', membership, weighted, precision=lax.P...  21.7 us
    convert_element_type x2, other arithmetic, local(): step_half = (2.0 * primal_next - primal).astype(jnp.bfloat16)  14.3 us
    reshape x2, local copies, waits for them, and re-layouts, local(): adjoint = placed.reshape(scenario_count, local_sections, columns)  13.4 us
    unnamed x45, local copies, waits for them, and re-layouts  12.2 us
  transfers between devices with their start and end apart: 4, of which 2 were waited for; matrix products, arithmetic and copies ran while one was open for 13% of the time, Pallas kernels for 0%

profile of v1, /device:TPU:0, one launch (start us, length us, event | category | flops | bytes accessed | tf_op | source)
XLA Modules:
  0.0 330.5 jit_solution(9752587330020329745)
XLA Ops:
  7.3 0.9 convert_bitcast_fusion.1
  8.1 0.9 copy-done
  9.1 1.1 fusion.14
  10.2 2.9 collective-permute-start
  14.5 21.7 %psum.67 = f32[585]{0:T(1024)S(1)} all-reduce(f32[585]{0:T(1024)S(1)} %convolution_reduce_fusion), channel_id=1, replica_groups=mesh['scen'=8,'rows'=2,'section'=2] {'scen'}, use_global_device_ids=true, to_apply=%region_2.3 | all-reduce | flops 585 | bytes 4680 | tf_op jit(solution)/shard_map/psum | solution.py:112
  36.8 4.4 %copy_convert_fusion = f32[24,2,22528]{2,0,1:T(8,128)} fusion(bf16[24,2,22528]{2,1,0:T(2,128)(2,1)} %param.17), kind=kLoop, calls=%fused_computation.26 | loop fusion | flops 1081344 | bytes 6488064 | tf_op jit(solution)/shard_map/convert_element_type | solution.py:75
  41.2 6.6 %fusion.53 = f32[24,2,176,128]{3,2,1,0:T(8,128)} fusion(f32[24,2,2,128]{3,2,1,0:T(2,128)} %bitcast.4, pred[24,2,2,2,176]{4,3,2,0,1:T(4,128)(4,1)S(1)} %iota_compare_fusion, s32[]{:T(128)S(6)} %select_n.33), kind=kOutput, calls=%fused_computation.54 | convolution fusion | flops 25952256 | bytes 4423684 | tf_op jit(solution)/shard_map/srjnc,srjnb->sjcb/dot_general | solution.py:87
  47.8 1.5 fusion.57
  49.8 8.1 %convolution_add_fusion.1 = f32[24,2,176,128]{3,2,1,0:T(8,128)} fusion(f32[24,2,176,128]{3,2,1,0:T(8,128)} %fusion.53, pred[24,2,2,2,176]{4,3,2,0,1:T(4,128)(4,1)S(1)} %iota_compare_fusion, s32[]{:T(128)S(6)} %select_n.35, f32[24,1,2,2,128]{4,3,2,0,1:T(2,128)} %collective-permute-done), kind=kOutput, calls=%fused_computation.21 | convolution fusion | flops 27033600 | bytes 8749060 | tf_op jit(solution)/shard_map/srjnc,srjnb->sjcb/dot_general | solution.py:87
  57.9 6.7 %reshape.86 = f32[24,2,22528]{2,1,0:T(2,128)} reshape(f32[24,2,176,128]{3,2,1,0:T(8,128)} %convolution_add_fusion.1) | data formatting | bytes 8650752 | tf_op jit(solution)/shard_map/reshape | solution.py:94
  64.6 7.5 %subtract_convert_fusion.1 = (bf16[24,2,22528]{2,0,1:T(8,128)(2,1)S(1)}, f32[24,2,22528]{2,0,1:T(8,128)}) fusion(bf16[24,2,22528]{2,1,0:T(2,128)(2,1)} %param.17, f32[24,2,512]{2,0,1:T(8,128)S(1)} %get-tuple-element.25, f32[24,2,22528]{2,1,0:T(2,128)} %reshape.86, bf16[24,2,22528]{2,1,0:T(2,128)(2,1)} %param.15), kind=kLoop, calls=%fused_computation.11 | loop fusion | flops 10813440 | bytes 15237120 | tf_op jit(solution)/shard_map/convert_element_type | solution.py:98
  73.1 0.9 fusion.12
  74.0 3.3 psum.66
  77.3 2.7 convolution_bitcast_fusion.1
  81.2 3.8 %fusion.51 = f32[24,2,176,128]{3,2,1,0:T(8,128)S(1)} fusion(f32[24,2,2,128]{3,2,1,0:T(2,128)S(1)} %bitcast.117, pred[24,2,2,2,176]{4,3,2,0,1:T(4,128)(4,1)S(1)} %iota_compare_fusion, s32[]{:T(128)S(6)} %select_n.33), kind=kOutput, calls=%fused_computation.52 | convolution fusion | flops 25952256 | bytes 4423684 | tf_op jit(solution)/shard_map/srjnc,srjnb->sjcb/dot_general | solution.py:87
  85.0 5.6 %convolution_add_fusion = f32[24,2,176,128]{3,2,1,0:T(8,128)} fusion(f32[24,2,176,128]{3,2,1,0:T(8,128)S(1)} %fusion.51, pred[24,2,2,2,176]{4,3,2,0,1:T(4,128)(4,1)S(1)} %iota_compare_fusion, s32[]{:T(128)S(6)} %select_n.35, f32[24,1,2,2,128]{4,3,2,0,1:T(2,128)S(1)} %collective-permute-done.1), kind=kOutput, calls=%fused_computation.20 | convolution fusion | flops 27033600 | bytes 8749060 | tf_op jit(solution)/shard_map/srjnc,srjnb->sjcb/dot_general | solution.py:87
  90.6 6.7 %reshape.115 = f32[24,2,22528]{2,1,0:T(2,128)} reshape(f32[24,2,176,128]{3,2,1,0:T(8,128)} %convolution_add_fusion) | data formatting | bytes 8650752 | tf_op jit(solution)/shard_map/reshape | solution.py:94
  97.3 60.4 %all-reduce.8.cloned.1.call-done = f32[585,512]{1,0:T(8,128)} async-done(((f32[585,512]{1,0:T(8,128)}), f32[585,512]{1,0:T(8,128)}) %all-reduce.8.cloned.1.call-update) | async-done | bytes 1198096 | tf_op jit(solution)/shard_map/psum | solution.py:112
  157.7 2.1 fusion.25
  159.8 1.6 multiply_reduce_fusion.2
  161.4 31.8 %all-reduce.4 = (f32[]{:T(128)}, f32[]{:T(128)}) all-reduce(f32[]{:T(128)} %get-tuple-element.15, f32[]{:T(128)} %get-tuple-element.14), channel_id=1, replica_groups=mesh['scen'=8,'rows'=2,'section'=2] {'scen','section'}, use_global_device_ids=true, to_apply=%region_5.6 | all-reduce | flops 2 | bytes 16 | tf_op jit(solution)/shard_map/psum | solution.py:125
  194.6 0.9 multiply_add_fusion.1
  195.5 6.8 %subtract_convert_fusion = (bf16[24,2,22528]{2,0,1:T(8,128)(2,1)}, f32[24,2,22528]{2,0,1:T(8,128)S(1)}) fusion(f32[24,2,22528]{2,0,1:T(8,128)} %get-tuple-element.23, f32[24,2,512]{2,0,1:T(8,128)S(1)} %multiply_add_fusion.1, f32[24,2,22528]{2,1,0:T(2,128)} %reshape.115, bf16[24,2,22528]{2,1,0:T(2,128)(2,1)} %param.15), kind=kLoop, calls=%fused_computation.10 | loop fusion | flops 9732096 | bytes 17399808 | tf_op jit(solution)/shard_map/convert_element_type | solution.py:98
  202.3 2.0 copy-done.1
  204.3 1.8 convolution_bitcast_fusion
  206.2 7.8 %copy.35 = f32[24,2,22528]{2,1,0:T(2,128)} copy(f32[24,2,22528]{2,0,1:T(8,128)} %copy-done.1) | data formatting | bytes 8650752
  215.0 0.9 fusion.8
  215.9 3.3 psum.71
  219.8 65.0 %all-reduce.10.cloned.1.call-done = f32[585,512]{1,0:T(8,128)} async-done(((f32[585,512]{1,0:T(8,128)}), f32[585,512]{1,0:T(8,128)}) %all-reduce.10.cloned.1.call-update) | async-done | bytes 1198096 | tf_op jit(solution)/shard_map/psum | solution.py:112
  284.8 2.1 fusion.22
  286.9 1.7 multiply_reduce_fusion
  289.2 31.9 %all-reduce.3 = (f32[]{:T(128)}, f32[]{:T(128)}) all-reduce(f32[]{:T(128)} %get-tuple-element.13, f32[]{:T(128)} %get-tuple-element.12), channel_id=1, replica_groups=mesh['scen'=8,'rows'=2,'section'=2] {'scen','section'}, use_global_device_ids=true, to_apply=%region_11.12 | all-reduce | flops 2 | bytes 16 | tf_op jit(solution)/shard_map/psum | solution.py:125
  (62 shorter events, 7.0 us)
Async XLA Ops:
  7.2 1.9 copy-start
  7.2 6.0 %copy-start.19 = (s32[3]{0:T(128)S(1)}, s32[3]{0:T(128)}, u32[]{:S(2)}) copy-start(s32[3]{0:T(128)} %constant.43.clone) | copy-start | bytes 40
  7.2 6.0 %copy-start.17 = (s32[3,24]{1,0:T(4,128)S(1)}, s32[3,24]{1,0:T(4,128)}, u32[]{:S(2)}) copy-start(s32[3,24]{1,0:T(4,128)} %param.13) | copy-start | bytes 868
  7.2 6.8 %copy-start.16 = (s32[24,2,2,2]{0,3,2,1:T(2,128)S(1)}, s32[24,2,2,2]{0,3,2,1:T(2,128)}, u32[]{:S(2)}) copy-start(s32[24,2,2,2]{0,3,2,1:T(2,128)} %param.12) | copy-start | bytes 2308
  7.2 7.1 %copy-start.11 = (f32[24]{0:T(128)S(1)}, f32[24]{0:T(128)}, u32[]{:S(2)}) copy-start(f32[24]{0:T(128)} %param.14) | copy-start | bytes 292
  7.2 150.5 %all-reduce.8.cloned.1.call-start = ((), (), s32[]{:S(2)}) async-start(), calls=%async_computation | async-start | bytes 2424832 | tf_op jit(solution)/shard_map/psum | solution.py:112
  10.2 39.6 %collective-permute-start = (f32[24,1,2,2,128]{4,3,2,0,1:T(2,128)}, f32[24,1,2,2,128]{4,3,2,0,1:T(2,128)}, u32[]{:S(2)}, u32[]{:S(2)}) collective-permute-start(f32[24,1,2,2,128]{4,3,2,0,1:T(2,128)} %bitcast.6), channel_id=1, source_target_pairs={{0,2},{2,0},{1,3},{3,1},{4,6},{6,4},{5,7},{7,5},{8,10},{10,8},{9,1... | collective-permute-start | bytes 147464 | tf_op jit(solution)/shard_map/ppermute | solution.py:25
  41.2 6.6 %copy-start.4 = (f32[24,2,512]{2,1,0:T(2,128)S(1)}, f32[24,2,512]{2,1,0:T(2,128)}, u32[]{:S(2)}) copy-start(f32[24,2,512]{2,1,0:T(2,128)} %param.19) | copy-start | bytes 294916
  41.2 6.6 %copy-start.3 = (f32[585,512]{1,0:T(8,128)S(1)}, f32[585,512]{1,0:T(8,128)}, u32[]{:S(2)}) copy-start(f32[585,512]{1,0:T(8,128)} %param.20) | copy-start | bytes 3594244
  72.4 4.9 %copy-start.12 = (f32[24]{0:T(128)S(1)}, f32[24]{0:T(128)}, u32[]{:S(2)}) copy-start(f32[24]{0:T(128)} %param.14) | copy-start | bytes 292
  73.1 7.0 %copy-start.5 = (f32[24,128]{1,0:T(8,128)S(1)}, f32[24,128]{1,0:T(8,128)}, u32[]{:S(2)}) copy-start(f32[24,128]{1,0:T(8,128)} %param.18) | copy-start | bytes 36868
  73.1 7.0 %copy-start.8 = (f32[24,128]{1,0:T(8,128)S(1)}, f32[24,128]{1,0:T(8,128)}, u32[]{:S(2)}) copy-start(f32[24,128]{1,0:T(8,128)} %param.16) | copy-start | bytes 36868
  77.3 2.8 copy-start.6
  80.0 204.8 %all-reduce.10.cloned.1.call-start = ((), (), s32[]{:S(2)}) async-start(), calls=%async_computation.1 | async-start | bytes 2424832 | tf_op jit(solution)/shard_map/psum | solution.py:112
  80.6 4.3 %collective-permute-start.1 = (f32[24,1,2,2,128]{4,3,2,0,1:T(2,128)S(1)}, f32[24,1,2,2,128]{4,3,2,0,1:T(2,128)S(1)}, u32[]{:S(2)}, u32[]{:S(2)}) collective-permute-start(f32[24,1,2,2,128]{4,3,2,0,1:T(2,128)S(1)} %bitcast.116), channel_id=1, source_target_pairs={{0,2},{2,0},{1,3},{3,1},{4,6},{6,4},{5,7},{7,5},{8,10},{10,8},{9,1... | collective-permute-start | bytes 147464 | tf_op jit(solution)/shard_map/ppermute | solution.py:25
  157.7 2.1 copy-start.13
  195.5 8.8 %copy-start.14 = (f32[24]{0:T(128)S(1)}, f32[24]{0:T(128)}, u32[]{:S(2)}) copy-start(f32[24]{0:T(128)} %param.14) | copy-start | bytes 292
  202.3 2.0 copy-start.1
  206.1 7.8 %copy-start.2 = (bf16[24,2,22528]{2,0,1:T(8,128)(2,1)S(1)}, bf16[24,2,22528]{2,0,1:T(8,128)(2,1)}, u32[]{:S(2)}) copy-start(bf16[24,2,22528]{2,0,1:T(8,128)(2,1)} %get-tuple-element.20) | copy-start | bytes 6488068
  214.2 4.9 %copy-start.7 = (f32[24,128]{1,0:T(8,128)S(1)}, f32[24,128]{1,0:T(8,128)}, u32[]{:S(2)}) copy-start(f32[24,128]{1,0:T(8,128)} %copy-done.6) | copy-start | bytes 36868
  214.2 4.9 %copy-start.9 = (f32[24,128]{1,0:T(8,128)S(1)}, f32[24,128]{1,0:T(8,128)}, u32[]{:S(2)}) copy-start(f32[24,128]{1,0:T(8,128)} %param.16) | copy-start | bytes 36868
  214.3 70.5 %copy-start.10 = (pred[2,585,24]{1,2,0:T(8,128)(4,1)S(1)}, pred[2,585,24]{1,2,0:T(8,128)(4,1)}, u32[]{:S(2)}) copy-start(pred[2,585,24]{1,2,0:T(8,128)(4,1)} %iota_compare_fusion.1) | copy-start | bytes 84244
  214.3 70.5 %copy-start.15 = (f32[585]{0:T(1024)S(1)}, f32[585]{0:T(1024)}, u32[]{:S(2)}) copy-start(f32[585]{0:T(1024)} %broadcast_select_fusion) | copy-start | bytes 7024
  214.9 69.8 %copy-start.18 = (pred[585]{0:T(1024)(128)(4,1)S(1)}, pred[585]{0:T(1024)(128)(4,1)}, u32[]{:S(2)}) copy-start(pred[585]{0:T(1024)(128)(4,1)} %broadcast_compare_fusion) | copy-start | bytes 1759
Sparse Core Ops, SparseCore 0:
  80.1 77.5 all-reduce.7
  206.3 78.4 all-reduce.9
